TPU v7x, 128 devices: a whole 4x4x4 slice. The times are simulated.
128 devices in a mesh: row: 8 (over x, z_hi), col: 16 (over y, z_lo, core).
Axes of the slice: x: 4, y: 4, z: 4 (z_hi: 2, z_lo: 2; z = z_hi * 2 + z_lo), core: 2. Of those that a mesh axis runs over, the one named last changes fastest.
Arguments:
- residual: bfloat16 [256, 5120], P('row', 'col'), may hold values from -6 to 6
- attn_gain: float32 [5120], P('col'), may hold values from 0.1 to 1.9
- w_query: bfloat16 [5120, 5120], P('col', 'row'), may hold values from -0.078125 to 0.078125
- w_key: bfloat16 [5120, 1024], P('col', 'row'), may hold values from -0.078125 to 0.078125
- w_value: bfloat16 [5120, 1024], P('col', 'row'), may hold values from -0.078125 to 0.078125
- w_out: bfloat16 [5120, 5120], P('row', 'col'), may hold values from -0.078125 to 0.078125
- mlp_gain: float32 [5120], P('col'), may hold values from 0.1 to 1.9
- w_gate: bfloat16 [2, 5120, 13824], P(None, 'col', 'row'), may hold values from -0.078125 to 0.078125
- w_up: bfloat16 [2, 5120, 13824], P(None, 'col', 'row'), may hold values from -0.078125 to 0.078125
- w_down: bfloat16 [2, 13824, 5120], P(None, 'row', 'col'), may hold values from -0.0546875 to 0.0546875
- final_gain: float32 [5120], P('col'), may hold values from 0.1 to 1.9
- w_head: bfloat16 [5120, 81920], P(None, ('row', 'col')), may hold values from -32 to 32
- seq_lengths: int32 [8], replicated, may hold values from 1 to 64, 256 in all
- targets: int32 [256], replicated, may hold values from 0 to 81919
Outputs:
- seq_diff: float32 [8], replicated
Inputs may be any that keep to these rules, and one draw needn't show every extreme that they name: `seq_lengths`: the lengths sum to 256 and the largest is exactly 64.
All inputs are finite; a program needn't handle non-finite values.
Results may differ from a plain program's by a relative error of at most 0.02.
Values may be sent and summed in bfloat16 or wider, within the bound.
A program may use at most 64 MiB of HBM per device.

v0:
```python
import jax
import jax.numpy as jnp
from jax import lax
from jax.sharding import PartitionSpec as P

D = 5120
HEAD_DIM = 128
SEQS = 8
EPSILON = 1e-06
ROPE_BASE = 1000000.0
MASKED = -1e30


def sequence_layout(seq_lengths, token_index):
    ends_at = jnp.cumsum(seq_lengths)
    before = ends_at[None, :] <= token_index[:, None]
    segment = jnp.sum(before.astype(jnp.int32), axis=1)
    starts_at = jnp.sum(jnp.where(before, seq_lengths[None, :], 0), axis=1)
    return (segment, (token_index - starts_at).astype(jnp.float32))


def angles_for(positions, head_width):
    exponent = jnp.arange(head_width // 2, dtype=jnp.float32) * 2.0 / head_width
    frequency = ROPE_BASE ** (-exponent)
    return positions[:, None] * frequency[None, :]


def rotate(features, angles):
    half_width = features.shape[-1] // 2
    lower_half = features[..., :half_width]
    upper_half = features[..., half_width:]
    cosine = jnp.cos(angles)[:, None, :]
    sine_part = jnp.sin(angles)[:, None, :]
    return jnp.concatenate(
        [
            lower_half * cosine - upper_half * sine_part,
            upper_half * cosine + lower_half * sine_part,
        ],
        axis=-1,
    )


def rms_local(features, gain_vector):
    squares = jnp.sum(features * features, axis=1)
    grand_total = lax.psum(squares, "col")
    return features * lax.rsqrt(grand_total / D + EPSILON)[:, None] * gain_vector[None, :]


def feed_forward(mlp_input, gate_up, down_weight):
    ff_local = down_weight.shape[0]
    row_block = mlp_input
    summed = lax.psum_scatter(
        jnp.dot(row_block, gate_up, preferred_element_type=jnp.float32),
        "col",
        scatter_dimension=0,
        tiled=True,
    )
    hidden = (jax.nn.silu(summed[:, :ff_local]) * summed[:, ff_local:]).astype(jnp.bfloat16)
    hidden_all = lax.all_gather(hidden, "col", axis=0, tiled=True)
    row_block = hidden_all
    return lax.psum_scatter(
        jnp.dot(row_block, down_weight, preferred_element_type=jnp.float32),
        "row",
        scatter_dimension=0,
        tiled=True,
    )


def per_device(
    residual,
    attn_gain,
    w_query,
    w_key,
    w_value,
    w_out,
    mlp_gain,
    w_gate,
    w_up,
    w_down,
    final_gain,
    w_head,
    seq_lengths,
    targets,
):
    row_count = lax.axis_size("row")
    col_count = lax.axis_size("col")
    row_index = lax.axis_index("row")
    col_index = lax.axis_index("col")
    local_rows = residual.shape[0]
    total_tokens = local_rows * row_count
    query_heads = w_query.shape[1] // HEAD_DIM
    kv_local = w_key.shape[1] // HEAD_DIM
    group_size = query_heads // kv_local
    query_width = query_heads * HEAD_DIM
    key_width = kv_local * HEAD_DIM
    stream_in = residual.astype(jnp.float32)
    normed = rms_local(stream_in, attn_gain).astype(jnp.bfloat16)
    gathered = lax.all_gather(normed, "row", axis=0, tiled=True)
    w_joint = jnp.concatenate([w_query, w_key, w_value], axis=1)
    joint_part = jnp.dot(gathered, w_joint, preferred_element_type=jnp.float32)
    joint_sums = lax.psum(joint_part, "col")
    token_index = jnp.arange(total_tokens, dtype=jnp.int32)
    segment, positions = sequence_layout(seq_lengths, token_index)
    angles = angles_for(positions, HEAD_DIM)
    queries = rotate(
        joint_sums[:, :query_width].reshape(total_tokens, query_heads, HEAD_DIM), angles
    ).astype(jnp.bfloat16)
    keys_all = rotate(
        joint_sums[:, query_width : query_width + key_width].reshape(
            total_tokens, kv_local, HEAD_DIM
        ),
        angles,
    ).astype(jnp.bfloat16)
    values_all = (
        joint_sums[:, query_width + key_width :]
        .astype(jnp.bfloat16)
        .reshape(total_tokens, kv_local, HEAD_DIM)
    )
    grouped = queries.reshape(total_tokens, kv_local, group_size, HEAD_DIM)
    block_rows = min(512, total_tokens)
    block_count = total_tokens // block_rows

    def attend_block(block_start):
        block_index = block_start + jnp.arange(block_rows, dtype=jnp.int32)
        scores = jnp.einsum(
            "qhgd,khd->hgqk", grouped, keys_all, preferred_element_type=jnp.float32
        ) * HEAD_DIM ** (-0.5)
        allowed = (segment[:, None] == segment[None, :]) & (
            token_index[None, :] <= block_index[:, None]
        )
        scores = jnp.where(allowed[None, None], scores, MASKED)
        top_value = jnp.max(scores, axis=-1, keepdims=True)
        weights = jnp.exp(scores - top_value)
        weights = (weights / jnp.sum(weights, axis=-1, keepdims=True)).astype(jnp.bfloat16)
        result = jnp.einsum(
            "hgqk,khd->qhgd", weights, values_all, preferred_element_type=jnp.float32
        )
        return result.astype(jnp.bfloat16).reshape(block_rows, query_width)

    block_starts = jnp.arange(block_count, dtype=jnp.int32) * block_rows
    attn_all = lax.map(attend_block, block_starts).reshape(total_tokens, query_width)
    projected = lax.psum_scatter(
        jnp.dot(attn_all, w_out, preferred_element_type=jnp.float32),
        "row",
        scatter_dimension=0,
        tiled=True,
    )
    stream = lax.optimization_barrier((stream_in + projected).astype(jnp.bfloat16))
    stream_f = stream.astype(jnp.float32)
    mlp_in = rms_local(stream_f, mlp_gain).astype(jnp.bfloat16)
    mlp_input = lax.all_gather(mlp_in, "row", axis=0, tiled=True)
    outputs = []
    for member in range(2):
        gate_up = jnp.concatenate([w_gate[member], w_up[member]], axis=1)
        outputs.append(stream_f + feed_forward(mlp_input, gate_up, w_down[member]))
    pair_sums = lax.psum(
        (jnp.sum(outputs[0] * outputs[0], axis=1), jnp.sum(outputs[1] * outputs[1], axis=1)), "col"
    )
    policy_final = (
        outputs[0] * lax.rsqrt(pair_sums[0] / D + EPSILON)[:, None] * final_gain[None, :]
    ).astype(jnp.bfloat16)
    refer_final = (
        outputs[1] * lax.rsqrt(pair_sums[1] / D + EPSILON)[:, None] * final_gain[None, :]
    ).astype(jnp.bfloat16)
    wide_pair = (
        lax.all_gather(policy_final, "col", axis=1, tiled=True),
        lax.all_gather(refer_final, "col", axis=1, tiled=True),
    )
    policy_all, refer_all = (
        lax.all_gather(wide_pair[0], "row", axis=0, tiled=True),
        lax.all_gather(wide_pair[1], "row", axis=0, tiled=True),
    )
    vocab_local = w_head.shape[1]
    vocab_start = (row_index * col_count + col_index) * vocab_local
    vocab_ids = vocab_start + jnp.arange(vocab_local, dtype=jnp.int32)
    target_hits = targets[:, None] == vocab_ids[None, :]

    def local_stats(final_all):
        logits = jnp.dot(final_all, w_head, preferred_element_type=jnp.float32)
        local_top = jnp.max(logits, axis=1)
        local_total = jnp.sum(jnp.exp(logits - local_top[:, None]), axis=1)
        picked = jnp.sum(jnp.where(target_hits, logits, 0.0), axis=1)
        return (local_top, local_total, picked)

    policy_top, policy_total, policy_picked = local_stats(policy_all)
    refer_top, refer_total, refer_picked = local_stats(refer_all)
    top_policy, top_refer = lax.pmax((policy_top, refer_top), ("row", "col"))
    vocab_sums = lax.psum(
        (
            policy_total * jnp.exp(policy_top - top_policy),
            refer_total * jnp.exp(refer_top - top_refer),
            policy_picked,
            refer_picked,
        ),
        ("row", "col"),
    )
    policy_logprob = vocab_sums[2] - (top_policy + jnp.log(vocab_sums[0]))
    refer_logprob = vocab_sums[3] - (top_refer + jnp.log(vocab_sums[1]))
    difference = policy_logprob - refer_logprob
    one_hot = (segment[:, None] == jnp.arange(SEQS, dtype=jnp.int32)[None, :]).astype(jnp.float32)
    seq_sums = jnp.dot(difference, one_hot, precision=lax.Precision.HIGHEST)
    return seq_sums / seq_lengths.astype(jnp.float32)


def solution(mesh):
    placed = (
        P("row", "col"),
        P("col"),
        P("col", "row"),
        P("col", "row"),
        P("col", "row"),
        P("row", "col"),
        P("col"),
        P(None, "col", "row"),
        P(None, "col", "row"),
        P(None, "row", "col"),
        P("col"),
        P(None, ("row", "col")),
        P(),
        P(),
    )
    return jax.shard_map(per_device, mesh=mesh, in_specs=placed, out_specs=P(), check_vma=False)
```

profile of v0, /device:TPU:1, one launch (start us, length us, event | category | flops | bytes accessed | tf_op | source)
XLA Modules:
  0.0 926.4 jit_solution(10719453309221844499)
XLA Ops:
  7.5 28.6 %psum.63 = f32[32]{0:T(128)S(1)} all-reduce(f32[32]{0:T(128)S(1)} %fusion.48), channel_id=1, replica_groups=mesh['row'=8,'col'=16] {'col'}, use_global_device_ids=true, to_apply=%region_1.0 | all-reduce | flops 32 | bytes 256 | tf_op jit(solution)/shard_map/psum | solution.py:45
  36.9 28.5 %all_gather.24 = bf16[256,320]{1,0:T(8,128)(2,1)S(1)} all-gather(bf16[32,320]{1,0:T(8,128)(2,1)S(1)} %fusion.50), channel_id=1, replica_groups=mesh['row'=8,'col'=16] {'row'}, dimensions={0}, use_global_device_ids=true | all-gather | bytes 184320 | tf_op jit(solution)/shard_map/all_gather | solution.py:98
  65.4 2.5 fusion.21
  68.9 126.3 %all-reduce.5.cloned.1.call-done = f32[256,896]{1,0:T(8,128)} async-done(((f32[256,896]{1,0:T(8,128)}), f32[256,896]{1,0:T(8,128)}) %all-reduce.5.cloned.1.call-update) | async-done | bytes 917520 | tf_op jit(solution)/shard_map/psum | solution.py:101
  195.2 1.1 slice.73
  199.4 1.3 convolution_convert_fusion
  200.7 1.1 fusion.65
  202.0 4.0 slice_bitcast_fusion.2
  206.0 66.2 %reduce-scatter.6.cloned.1.call-done = f32[32,320]{1,0:T(8,128)} async-done(((f32[256,320]{1,0:T(8,128)}), f32[32,320]{1,0:T(8,128)}) %reduce-scatter.6.cloned.1.call-update) | async-done | bytes 40976 | tf_op jit(solution)/shard_map/reduce_scatter | solution.py:142
  273.0 29.0 %psum.65 = f32[32]{0:T(128)S(1)} all-reduce(f32[32]{0:T(128)S(1)} %fusion.52), channel_id=1, replica_groups=mesh['row'=8,'col'=16] {'col'}, use_global_device_ids=true, to_apply=%region_10.11 | all-reduce | flops 32 | bytes 256 | tf_op jit(solution)/shard_map/psum | solution.py:45
  302.2 28.0 %all_gather.25 = bf16[256,320]{1,0:T(8,128)(2,1)S(1)} all-gather(bf16[32,320]{1,0:T(8,128)(2,1)S(1)} %fusion.54), channel_id=1, replica_groups=mesh['row'=8,'col'=16] {'row'}, dimensions={0}, use_global_device_ids=true | all-gather | bytes 184320 | tf_op jit(solution)/shard_map/all_gather | solution.py:151
  330.2 4.5 fusion.4
  334.8 2.9 fusion
  337.7 63.7 %reduce-scatter.12.cloned.1.call-done = f32[16,3456]{1,0:T(8,128)} async-done(((f32[256,3456]{1,0:T(8,128)}), f32[16,3456]{1,0:T(8,128)}) %reduce-scatter.12.cloned.1.call-update) | async-done | bytes 221200 | tf_op jit(solution)/shard_map/reduce_scatter | solution.py:52
  401.4 1.1 fusion.39
  402.5 24.7 %all_gather.29 = bf16[256,1728]{1,0:T(8,128)(2,1)S(1)} all-gather(bf16[16,1728]{1,0:T(8,128)(2,1)S(1)} %fusion.39), channel_id=1, replica_groups=mesh['row'=8,'col'=16] {'col'}, dimensions={0}, use_global_device_ids=true | all-gather | bytes 940032 | tf_op jit(solution)/shard_map/all_gather | solution.py:59
  427.2 1.4 fusion.11
  428.7 42.0 %reduce-scatter.8.cloned.1.call-done = f32[16,3456]{1,0:T(8,128)} async-done(((f32[256,3456]{1,0:T(8,128)}), f32[16,3456]{1,0:T(8,128)}) %reduce-scatter.8.cloned.1.call-update) | async-done | bytes 221200 | tf_op jit(solution)/shard_map/reduce_scatter | solution.py:52
  470.6 1.1 fusion.40
  471.7 21.1 %all_gather.26 = bf16[256,1728]{1,0:T(8,128)(2,1)S(1)} all-gather(bf16[16,1728]{1,0:T(8,128)(2,1)S(1)} %fusion.40), channel_id=1, replica_groups=mesh['row'=8,'col'=16] {'col'}, dimensions={0}, use_global_device_ids=true | all-gather | bytes 940032 | tf_op jit(solution)/shard_map/all_gather | solution.py:59
  492.8 1.4 fusion.13
  494.2 50.7 %reduce-scatter.14.cloned.1.call-done = f32[32,320]{1,0:T(8,128)} async-done(((f32[256,320]{1,0:T(8,128)}), f32[32,320]{1,0:T(8,128)}) %reduce-scatter.14.cloned.1.call-update) | async-done | bytes 40976 | tf_op jit(solution)/shard_map/reduce_scatter | solution.py:61
  545.0 74.0 %reduce-scatter.10.cloned.1.call-done = f32[32,320]{1,0:T(8,128)} async-done(((f32[256,320]{1,0:T(8,128)}), f32[32,320]{1,0:T(8,128)}) %reduce-scatter.10.cloned.1.call-update) | async-done | bytes 40976 | tf_op jit(solution)/shard_map/reduce_scatter | solution.py:61
  619.9 29.1 %all-reduce.2 = (f32[32]{0:T(128)S(1)}, f32[32]{0:T(128)S(1)}) all-reduce(f32[32]{0:T(128)S(1)} %get-tuple-element.30, f32[32]{0:T(128)S(1)} %get-tuple-element.28), channel_id=1, replica_groups=mesh['row'=8,'col'=16] {'col'}, use_global_device_ids=true, to_apply=%region_24.25 | all-reduce | flops 64 | bytes 512 | tf_op jit(solution)/shard_map/psum | solution.py:156
  649.9 18.1 %all-gather = bf16[16,320,32]{1,2,0:T(8,128)(2,1)S(1)} all-gather(bf16[1,320,32]{1,2,0:T(8,128)(2,1)S(1)} %get-tuple-element.52), channel_id=1, replica_groups=mesh['row'=8,'col'=16] {'col'}, dimensions={0}, use_global_device_ids=true | all-gather | bytes 348160 | tf_op jit(solution)/shard_map/all_gather | solution.py:166
  669.2 19.3 %all-gather.1 = bf16[16,320,32]{1,2,0:T(8,128)(2,1)S(1)} all-gather(bf16[1,320,32]{1,2,0:T(8,128)(2,1)S(1)} %get-tuple-element.53), channel_id=1, replica_groups=mesh['row'=8,'col'=16] {'col'}, dimensions={0}, use_global_device_ids=true | all-gather | bytes 348160 | tf_op jit(solution)/shard_map/all_gather | solution.py:167
  689.6 35.1 %all-gather.5.cloned.1.call-done = bf16[256,5120]{1,0:T(8,128)(2,1)} async-done(((bf16[32,5120]{1,0:T(8,128)(2,1)}), bf16[256,5120]{1,0:T(8,128)(2,1)}) %all-gather.5.cloned.1.call-update) | async-done | bytes 2621456 | tf_op jit(solution)/shard_map/all_gather | solution.py:170
  724.8 5.9 fusion.63
  730.7 54.1 %all-gather.7.cloned.1.call-done = bf16[256,5120]{1,0:T(8,128)(2,1)} async-done(((bf16[32,5120]{1,0:T(8,128)(2,1)}), bf16[256,5120]{1,0:T(8,128)(2,1)}) %all-gather.7.cloned.1.call-update) | async-done | bytes 2621456 | tf_op jit(solution)/shard_map/all_gather | solution.py:171
  784.9 5.9 fusion.64
  790.8 65.0 %all-reduce.1 = (f32[256]{0:T(256)S(1)}, f32[256]{0:T(256)S(1)}) all-reduce(f32[256]{0:T(256)S(1)} %get-tuple-element.62, f32[256]{0:T(256)S(1)} %get-tuple-element.60), channel_id=1, replica_groups=mesh['row'=8,'col'=16] {'row','col'}, use_global_device_ids=true, to_apply=%region_28.29 | all-reduce | flops 512 | bytes 4096 | tf_op jit(solution)/shard_map/pmax | solution.py:187
  856.3 62.5 %all-reduce = (f32[256]{0:T(256)S(1)}, f32[256]{0:T(256)S(1)}, f32[256]{0:T(256)S(1)}, f32[256]{0:T(256)S(1)}) all-reduce(f32[256]{0:T(256)S(1)} %get-tuple-element.54, f32[256]{0:T(256)S(1)} %exponential_multiply_fusion, f32[256]{0:T(256)S(1)} %get-tuple-element.18, ...), channel_id=1, replica_groups=mesh['row'=8,'col'=16] {'row','col'}, use_global_device_ids=true, to_apply=%region_26.27 | all-reduce | flops 1024 | bytes 8192 | tf_op jit(solution)/shard_map/psum | solution.py:188
  (66 shorter events, 12.6 us)
Async XLA Ops:
  6.5 194.2 %copy-start = (bf16[640,320]{0,1:T(8,128)(2,1)S(1)}, bf16[640,320]{0,1:T(8,128)(2,1)}, u32[]{:S(2)}) copy-start(bf16[640,320]{0,1:T(8,128)(2,1)} %param.19) | copy-start | bytes 1228804
  6.5 61.4 %copy-start.5 = (s32[8]{0:T(128)S(1)}, s32[8]{0:T(128)}, u32[]{:S(2)}) copy-start(s32[8]{0:T(128)} %param.26) | copy-start | bytes 100
  6.5 188.7 %all-reduce.5.cloned.1.call-start = ((), (), s32[]{:S(2)}) async-start(), calls=%async_computation.5 | async-start | bytes 1835008 | tf_op jit(solution)/shard_map/psum | solution.py:101
  67.9 204.2 %reduce-scatter.6.cloned.1.call-start = ((), (), s32[]{:S(2)}) async-start(), calls=%async_computation.6 | async-start | bytes 442368 | tf_op jit(solution)/shard_map/reduce_scatter | solution.py:142
  201.9 70.2 %copy-start.1 = (bf16[32,320]{1,0:T(8,128)(2,1)S(1)}, bf16[32,320]{1,0:T(8,128)(2,1)}, u32[]{:S(2)}) copy-start(bf16[32,320]{1,0:T(8,128)(2,1)} %param.14) | copy-start | bytes 61444
  201.9 100.2 %copy-start.3 = (f32[320]{0:T(512)S(1)}, f32[320]{0:T(512)}, u32[]{:S(2)}) copy-start(f32[320]{0:T(512)} %param.20) | copy-start | bytes 3844
  201.9 199.5 %reduce-scatter.12.cloned.1.call-start = ((), (), s32[]{:S(2)}) async-start(), calls=%async_computation.10 | async-start | bytes 3760128 | tf_op jit(solution)/shard_map/reduce_scatter | solution.py:52
  334.7 135.9 %reduce-scatter.8.cloned.1.call-start = ((), (), s32[]{:S(2)}) async-start(), calls=%async_computation.7 | async-start | bytes 3760128 | tf_op jit(solution)/shard_map/reduce_scatter | solution.py:52
  337.6 89.5 %copy-start.6 = (bf16[2,1728,320]{1,2,0:T(8,128)(2,1)S(1)}, bf16[2,1728,320]{1,2,0:T(8,128)(2,1)}, u32[]{:S(2)}) copy-start(bf16[2,1728,320]{1,2,0:T(8,128)(2,1)} %param.23) | copy-start | bytes 6635524
  337.7 207.3 %reduce-scatter.14.cloned.1.call-start = ((), (), s32[]{:S(2)}) async-start(), calls=%async_computation.11 | async-start | bytes 442368 | tf_op jit(solution)/shard_map/reduce_scatter | solution.py:61
  428.6 220.3 %copy-start.2 = (f32[320]{0:T(512)S(1)}, f32[320]{0:T(512)}, u32[]{:S(2)}) copy-start(f32[320]{0:T(512)} %param.24) | copy-start | bytes 3844
  428.6 190.3 %reduce-scatter.10.cloned.1.call-start = ((), (), s32[]{:S(2)}) async-start(), calls=%async_computation.8 | async-start | bytes 442368 | tf_op jit(solution)/shard_map/reduce_scatter | solution.py:61
  494.2 230.6 %all-gather.5.cloned.1.call-start = ((), (), s32[]{:S(2)}) async-start(), calls=%async_computation.9 | async-start | bytes 2949120 | tf_op jit(solution)/shard_map/all_gather | solution.py:170
  669.1 115.8 %all-gather.7.cloned.1.call-start = ((), (), s32[]{:S(2)}) async-start(), calls=%async_computation.12 | async-start | bytes 2949120 | tf_op jit(solution)/shard_map/all_gather | solution.py:171
  730.7 125.1 %copy-start.4 = (s32[256]{0:T(256)S(1)}, s32[256]{0:T(256)}, u32[]{:S(2)}) copy-start(s32[256]{0:T(256)} %param.27) | copy-start | bytes 3076
Sparse Core Ops, SparseCore 0:
  68.0 127.1 all-reduce.4
  202.0 70.0 reduce-scatter.5
  334.9 66.4 reduce-scatter.11
  403.8 66.7 reduce-scatter.7
  474.5 70.4 reduce-scatter.13
  548.8 70.0 reduce-scatter.9
  669.2 55.4 all-gather.4
  727.3 57.4 all-gather.6
where the time goes:
time: 927 us; the launch traced here: 926 us
  waiting for transfers between devices  512 us (55%)
  blocking collectives  354 us (38%)
  matrix products  28.1 us (3%)
  between operations  13.7 us (1%)
    psum x1, waiting for transfers between devices, per_device(): joint_sums = lax.psum(joint_part, 'col')  126 us
    reduce_scatter x2, waiting for transfers between devices, feed_forward(): lax.psum_scatter(jnp.dot(row_block, down_weight, preferred_element_type=j...  125 us
    reduce_scatter x2, waiting for transfers between devices, feed_forward(): lax.psum_scatter(jnp.dot(row_block, gate_up, preferred_element_type=jnp.f...  106 us
    reduce_scatter x1, waiting for transfers between devices, per_device(): lax.psum_scatter(jnp.dot(attn_all, w_out, preferred_element_type=jnp.floa...  66.2 us
    pmax x1, blocking collectives, per_device(): top_policy, top_refer = lax.pmax((policy_top, refer_top), ('row', 'col'))  65 us
    psum x1, blocking collectives, per_device(): lax.psum((policy_total * jnp.exp(policy_top - top_policy), refer_total *...  62.5 us
    psum x2, blocking collectives, rms_local(): grand_total = lax.psum(squares, 'col')  57.7 us
    all_gather x1, waiting for transfers between devices, per_device(): lax.all_gather(wide_pair[1], 'row', axis=0, tiled=True)  54.1 us
  transfers between devices with their start and end apart: 8, of which 8 were waited for; matrix products, arithmetic and copies ran while one was open for 2% of the time, Pallas kernels for 0%

commit v1 on v0

--- a/solution.py
+++ b/solution.py
@@ -98,7 +98,8 @@
     gathered = lax.all_gather(normed, "row", axis=0, tiled=True)
     w_joint = jnp.concatenate([w_query, w_key, w_value], axis=1)
     joint_part = jnp.dot(gathered, w_joint, preferred_element_type=jnp.float32)
-    joint_sums = lax.psum(joint_part, "col")
+    parts = lax.all_gather(joint_part, "col", axis=0, tiled=False)
+    joint_sums = parts.sum(axis=0)
     token_index = jnp.arange(total_tokens, dtype=jnp.int32)
     segment, positions = sequence_layout(seq_lengths, token_index)
     angles = angles_for(positions, HEAD_DIM)

time: 927 us -> 891 us (0.961)
  waiting for transfers between devices: 512 us -> 469 us
    psum x1 -> x0, waiting for transfers between devices: 126 us -> none  [per_device(): joint_sums = lax.psum(joint_part, 'col')]
    all_gather x0 -> x1, waiting for transfers between devices: none -> 89.4 us  [per_device(): parts = lax.all_gather(joint_part, 'col', axis=0, tiled=False)]
where the time goes in v1:
time: 891 us; the launch traced here: 890 us
  waiting for transfers between devices  469 us (53%)
  blocking collectives  358 us (40%)
  matrix products  27.1 us (3%)
  other arithmetic  15.1 us (2%)
  between operations  13.7 us (2%)
    reduce_scatter x2, waiting for transfers between devices, feed_forward(): lax.psum_scatter(jnp.dot(row_block, down_weight, preferred_element_type=j...  121 us
    reduce_scatter x2, waiting for transfers between devices, feed_forward(): lax.psum_scatter(jnp.dot(row_block, gate_up, preferred_element_type=jnp.f...  103 us
    all_gather x1, waiting for transfers between devices, per_device(): parts = lax.all_gather(joint_part, 'col', axis=0, tiled=False)  89.4 us
    reduce_scatter x1, waiting for transfers between devices, per_device(): lax.psum_scatter(jnp.dot(attn_all, w_out, preferred_element_type=jnp.floa...  65.6 us
    pmax x1, blocking collectives, per_device(): top_policy, top_refer = lax.pmax((policy_top, refer_top), ('row', 'col'))  65 us
    psum x1, blocking collectives, per_device(): lax.psum((policy_total * jnp.exp(policy_top - top_policy), refer_total *...  62.5 us
    psum x2, blocking collectives, rms_local(): grand_total = lax.psum(squares, 'col')  57.7 us
    all_gather x1, waiting for transfers between devices, per_device(): lax.all_gather(wide_pair[1], 'row', axis=0, tiled=True)  53.9 us
  transfers between devices with their start and end apart: 8, of which 8 were waited for; matrix products, arithmetic and copies ran while one was open for 2% of the time, Pallas kernels for 0%

profile of v1, /device:TPU:1, one launch (start us, length us, event | category | flops | bytes accessed | tf_op | source)
XLA Modules:
  0.0 890.3 jit_solution(5126902512493316714)
XLA Ops:
  7.5 28.6 %psum.56 = f32[32]{0:T(128)S(1)} all-reduce(f32[32]{0:T(128)S(1)} %fusion.48), channel_id=1, replica_groups=mesh['row'=8,'col'=16] {'col'}, use_global_device_ids=true, to_apply=%region_1.0 | all-reduce | flops 32 | bytes 256 | tf_op jit(solution)/shard_map/psum | solution.py:45
  36.9 28.5 %all_gather.30 = bf16[256,320]{1,0:T(8,128)(2,1)S(1)} all-gather(bf16[32,320]{1,0:T(8,128)(2,1)S(1)} %fusion.50), channel_id=1, replica_groups=mesh['row'=8,'col'=16] {'row'}, dimensions={0}, use_global_device_ids=true | all-gather | bytes 184320 | tf_op jit(solution)/shard_map/all_gather | solution.py:98
  65.4 2.4 fusion.21
  68.8 89.4 %all-gather.11.cloned.1.call-done = f32[4096,896]{1,0:T(8,128)} async-done(((f32[256,896]{1,0:T(8,128)}), f32[4096,896]{1,0:T(8,128)}) %all-gather.11.cloned.1.call-update) | async-done | bytes 14680080 | tf_op jit(solution)/shard_map/all_gather | solution.py:101
  158.2 5.9 reduce_sum.110
  166.8 1.1 fusion.65
  168.0 4.0 slice_bitcast_fusion.2
  172.1 65.6 %reduce-scatter.6.cloned.1.call-done = f32[32,320]{1,0:T(8,128)} async-done(((f32[256,320]{1,0:T(8,128)}), f32[32,320]{1,0:T(8,128)}) %reduce-scatter.6.cloned.1.call-update) | async-done | bytes 40976 | tf_op jit(solution)/shard_map/reduce_scatter | solution.py:143
  238.6 29.1 %psum.57 = f32[32]{0:T(128)S(1)} all-reduce(f32[32]{0:T(128)S(1)} %fusion.52), channel_id=1, replica_groups=mesh['row'=8,'col'=16] {'col'}, use_global_device_ids=true, to_apply=%region_10.11 | all-reduce | flops 32 | bytes 256 | tf_op jit(solution)/shard_map/psum | solution.py:45
  267.7 28.0 %all_gather.33 = bf16[256,320]{1,0:T(8,128)(2,1)S(1)} all-gather(bf16[32,320]{1,0:T(8,128)(2,1)S(1)} %fusion.54), channel_id=1, replica_groups=mesh['row'=8,'col'=16] {'row'}, dimensions={0}, use_global_device_ids=true | all-gather | bytes 184320 | tf_op jit(solution)/shard_map/all_gather | solution.py:152
  295.7 4.5 fusion
  300.3 2.9 fusion.4
  303.3 63.5 %reduce-scatter.8.cloned.1.call-done = f32[16,3456]{1,0:T(8,128)} async-done(((f32[256,3456]{1,0:T(8,128)}), f32[16,3456]{1,0:T(8,128)}) %reduce-scatter.8.cloned.1.call-update) | async-done | bytes 221200 | tf_op jit(solution)/shard_map/reduce_scatter | solution.py:52
  366.8 1.1 fusion.40
  367.9 26.2 %all_gather.34 = bf16[256,1728]{1,0:T(8,128)(2,1)S(1)} all-gather(bf16[16,1728]{1,0:T(8,128)(2,1)S(1)} %fusion.40), channel_id=1, replica_groups=mesh['row'=8,'col'=16] {'col'}, dimensions={0}, use_global_device_ids=true | all-gather | bytes 940032 | tf_op jit(solution)/shard_map/all_gather | solution.py:59
  394.1 1.4 fusion.13
  395.5 39.9 %reduce-scatter.12.cloned.1.call-done = f32[16,3456]{1,0:T(8,128)} async-done(((f32[256,3456]{1,0:T(8,128)}), f32[16,3456]{1,0:T(8,128)}) %reduce-scatter.12.cloned.1.call-update) | async-done | bytes 221200 | tf_op jit(solution)/shard_map/reduce_scatter | solution.py:52
  435.5 1.1 fusion.39
  436.6 23.9 %all_gather.37 = bf16[256,1728]{1,0:T(8,128)(2,1)S(1)} all-gather(bf16[16,1728]{1,0:T(8,128)(2,1)S(1)} %fusion.39), channel_id=1, replica_groups=mesh['row'=8,'col'=16] {'col'}, dimensions={0}, use_global_device_ids=true | all-gather | bytes 940032 | tf_op jit(solution)/shard_map/all_gather | solution.py:59
  460.4 1.4 fusion.11
  461.9 47.7 %reduce-scatter.10.cloned.1.call-done = f32[32,320]{1,0:T(8,128)} async-done(((f32[256,320]{1,0:T(8,128)}), f32[32,320]{1,0:T(8,128)}) %reduce-scatter.10.cloned.1.call-update) | async-done | bytes 40976 | tf_op jit(solution)/shard_map/reduce_scatter | solution.py:61
  509.7 73.5 %reduce-scatter.14.cloned.1.call-done = f32[32,320]{1,0:T(8,128)} async-done(((f32[256,320]{1,0:T(8,128)}), f32[32,320]{1,0:T(8,128)}) %reduce-scatter.14.cloned.1.call-update) | async-done | bytes 40976 | tf_op jit(solution)/shard_map/reduce_scatter | solution.py:61
  584.1 29.1 %all-reduce.2 = (f32[32]{0:T(128)S(1)}, f32[32]{0:T(128)S(1)}) all-reduce(f32[32]{0:T(128)S(1)} %get-tuple-element.30, f32[32]{0:T(128)S(1)} %get-tuple-element.28), channel_id=1, replica_groups=mesh['row'=8,'col'=16] {'col'}, use_global_device_ids=true, to_apply=%region_24.25 | all-reduce | flops 64 | bytes 512 | tf_op jit(solution)/shard_map/psum | solution.py:157
  614.1 18.1 %all-gather.1 = bf16[16,320,32]{1,2,0:T(8,128)(2,1)S(1)} all-gather(bf16[1,320,32]{1,2,0:T(8,128)(2,1)S(1)} %get-tuple-element.52), channel_id=1, replica_groups=mesh['row'=8,'col'=16] {'col'}, dimensions={0}, use_global_device_ids=true | all-gather | bytes 348160 | tf_op jit(solution)/shard_map/all_gather | solution.py:167
  633.4 19.3 %all-gather.2 = bf16[16,320,32]{1,2,0:T(8,128)(2,1)S(1)} all-gather(bf16[1,320,32]{1,2,0:T(8,128)(2,1)S(1)} %get-tuple-element.53), channel_id=1, replica_groups=mesh['row'=8,'col'=16] {'col'}, dimensions={0}, use_global_device_ids=true | all-gather | bytes 348160 | tf_op jit(solution)/shard_map/all_gather | solution.py:168
  652.8 1.0 reshape.258
  653.9 35.0 %all-gather.7.cloned.1.call-done = bf16[256,5120]{1,0:T(8,128)(2,1)} async-done(((bf16[32,5120]{1,0:T(8,128)(2,1)}), bf16[256,5120]{1,0:T(8,128)(2,1)}) %all-gather.7.cloned.1.call-update) | async-done | bytes 2621456 | tf_op jit(solution)/shard_map/all_gather | solution.py:171
  688.9 5.9 fusion.63
  694.9 53.9 %all-gather.9.cloned.1.call-done = bf16[256,5120]{1,0:T(8,128)(2,1)} async-done(((bf16[32,5120]{1,0:T(8,128)(2,1)}), bf16[256,5120]{1,0:T(8,128)(2,1)}) %all-gather.9.cloned.1.call-update) | async-done | bytes 2621456 | tf_op jit(solution)/shard_map/all_gather | solution.py:172
  748.7 5.9 fusion.64
  754.7 65.0 %all-reduce.1 = (f32[256]{0:T(256)S(1)}, f32[256]{0:T(256)S(1)}) all-reduce(f32[256]{0:T(256)S(1)} %get-tuple-element.62, f32[256]{0:T(256)S(1)} %get-tuple-element.60), channel_id=1, replica_groups=mesh['row'=8,'col'=16] {'row','col'}, use_global_device_ids=true, to_apply=%region_28.29 | all-reduce | flops 512 | bytes 4096 | tf_op jit(solution)/shard_map/pmax | solution.py:188
  820.1 62.5 %all-reduce = (f32[256]{0:T(256)S(1)}, f32[256]{0:T(256)S(1)}, f32[256]{0:T(256)S(1)}, f32[256]{0:T(256)S(1)}) all-reduce(f32[256]{0:T(256)S(1)} %get-tuple-element.54, f32[256]{0:T(256)S(1)} %exponential_multiply_fusion, f32[256]{0:T(256)S(1)} %get-tuple-element.18, ...), channel_id=1, replica_groups=mesh['row'=8,'col'=16] {'row','col'}, use_global_device_ids=true, to_apply=%region_26.27 | all-reduce | flops 1024 | bytes 8192 | tf_op jit(solution)/shard_map/psum | solution.py:189
  (67 shorter events, 11.1 us)
Async XLA Ops:
  6.5 160.3 %copy-start = (bf16[640,320]{0,1:T(8,128)(2,1)S(1)}, bf16[640,320]{0,1:T(8,128)(2,1)}, u32[]{:S(2)}) copy-start(bf16[640,320]{0,1:T(8,128)(2,1)} %param.19) | copy-start | bytes 1228804
  6.5 61.3 %copy-start.5 = (s32[8]{0:T(128)S(1)}, s32[8]{0:T(128)}, u32[]{:S(2)}) copy-start(s32[8]{0:T(128)} %param.26) | copy-start | bytes 100
  6.5 151.7 %all-gather.11.cloned.1.call-start = ((), (), s32[]{:S(2)}) async-start(), calls=%async_computation.12 | async-start | bytes 15597568 | tf_op jit(solution)/shard_map/all_gather | solution.py:101
  67.8 169.8 %reduce-scatter.6.cloned.1.call-start = ((), (), s32[]{:S(2)}) async-start(), calls=%async_computation.5 | async-start | bytes 442368 | tf_op jit(solution)/shard_map/reduce_scatter | solution.py:143
  168.0 69.7 %copy-start.1 = (bf16[32,320]{1,0:T(8,128)(2,1)S(1)}, bf16[32,320]{1,0:T(8,128)(2,1)}, u32[]{:S(2)}) copy-start(bf16[32,320]{1,0:T(8,128)(2,1)} %param.14) | copy-start | bytes 61444
  168.0 99.7 %copy-start.3 = (f32[320]{0:T(512)S(1)}, f32[320]{0:T(512)}, u32[]{:S(2)}) copy-start(f32[320]{0:T(512)} %param.20) | copy-start | bytes 3844
  168.0 198.8 %reduce-scatter.8.cloned.1.call-start = ((), (), s32[]{:S(2)}) async-start(), calls=%async_computation.6 | async-start | bytes 3760128 | tf_op jit(solution)/shard_map/reduce_scatter | solution.py:52
  300.2 135.3 %reduce-scatter.12.cloned.1.call-start = ((), (), s32[]{:S(2)}) async-start(), calls=%async_computation.9 | async-start | bytes 3760128 | tf_op jit(solution)/shard_map/reduce_scatter | solution.py:52
  303.2 90.9 %copy-start.6 = (bf16[2,1728,320]{1,2,0:T(8,128)(2,1)S(1)}, bf16[2,1728,320]{1,2,0:T(8,128)(2,1)}, u32[]{:S(2)}) copy-start(bf16[2,1728,320]{1,2,0:T(8,128)(2,1)} %param.23) | copy-start | bytes 6635524
  303.2 206.4 %reduce-scatter.10.cloned.1.call-start = ((), (), s32[]{:S(2)}) async-start(), calls=%async_computation.7 | async-start | bytes 442368 | tf_op jit(solution)/shard_map/reduce_scatter | solution.py:61
  395.5 217.7 %copy-start.2 = (f32[320]{0:T(512)S(1)}, f32[320]{0:T(512)}, u32[]{:S(2)}) copy-start(f32[320]{0:T(512)} %param.24) | copy-start | bytes 3844
  395.5 187.7 %reduce-scatter.14.cloned.1.call-start = ((), (), s32[]{:S(2)}) async-start(), calls=%async_computation.10 | async-start | bytes 442368 | tf_op jit(solution)/shard_map/reduce_scatter | solution.py:61
  461.9 227.0 %all-gather.7.cloned.1.call-start = ((), (), s32[]{:S(2)}) async-start(), calls=%async_computation.8 | async-start | bytes 2949120 | tf_op jit(solution)/shard_map/all_gather | solution.py:171
  633.3 115.4 %all-gather.9.cloned.1.call-start = ((), (), s32[]{:S(2)}) async-start(), calls=%async_computation.11 | async-start | bytes 2949120 | tf_op jit(solution)/shard_map/all_gather | solution.py:172
  694.8 124.8 %copy-start.4 = (s32[256]{0:T(256)S(1)}, s32[256]{0:T(256)}, u32[]{:S(2)}) copy-start(s32[256]{0:T(256)} %param.27) | copy-start | bytes 3076
Sparse Core Ops, SparseCore 0:
  68.0 90.2 all-gather.10
  168.1 69.5 reduce-scatter.5
  300.3 66.3 reduce-scatter.7
  369.1 66.3 reduce-scatter.11
  438.9 70.6 reduce-scatter.9
  513.1 70.0 reduce-scatter.13
  633.5 55.4 all-gather.6
  691.2 57.4 all-gather.8
